TPU v7x, 768 devices: a whole 4x8x12 slice. The times are simulated.
768 devices in a mesh: dp: 48 (over z_lo, y), fsdp: 16 (over x, z_hi, core).
Axes of the slice: x: 4, y: 8, z: 12 (z_hi: 2, z_lo: 6; z = z_hi * 6 + z_lo), core: 2. Of those that a mesh axis runs over, the one named last changes fastest.
Arguments:
- hidden_in: bfloat16 [98304, 14336], P(('dp', 'fsdp')), may hold values from -6 to 6
- out_grads: bfloat16 [98304, 4096], P(('dp', 'fsdp')), may hold values from -6 to 6
- piece_of: int32 [768, 128], P(('dp', 'fsdp')), may hold values from 0 to 47, never falling along the last dimension, each value on 1 to 5 neighbouring positions
- owner_dp: int32 [768, 48], P(('dp', 'fsdp')), may hold values from 0 to 47, as said below
- owner_slot: int32 [768, 48], P(('dp', 'fsdp')), may hold values from 0 to 23
- sketch_in: bfloat16 [14336, 64], P('fsdp'), may hold values from -0.046875 to 0.046875
- sketch_out: bfloat16 [4096, 64], P('fsdp'), may hold values from -0.09375 to 0.09375
Outputs:
- gram: float32 [192, 4096], P('dp', 'fsdp')
Inputs may be any that keep to these rules, and one draw needn't show every extreme that they name: `owner_dp`: each device sends exactly 2 pieces to each of 24 cyclically consecutive dp indices and none to the others; the first of these dp indices is the sender's dp index plus an offset that is the same for all devices that share an fsdp index, modulo 48.
All inputs are finite; a program needn't handle non-finite values.
Results may differ from a plain program's by a relative error of at most 0.0036.
Values may be sent and summed in bfloat16 or wider, within the bound.
A program may use at most 32 MiB of HBM per device.

v0:
```python
import math

import jax
import jax.numpy as jnp
from jax import lax
from jax.sharding import PartitionSpec as P

CAP = 2
GR = 192


def on_device(hidden_in, out_grads, piece_of, owner_dp, owner_slot, sketch_in, sketch_out):
    count_dp = lax.axis_size("dp")
    count_fsdp = lax.axis_size("fsdp")
    full_in, full_out = (
        lax.all_gather(sketch_in, "fsdp", axis=0, tiled=True),
        lax.all_gather(sketch_out, "fsdp", axis=0, tiled=True),
    )
    inputs_low = jnp.dot(hidden_in, full_in, preferred_element_type=jnp.float32).astype(
        jnp.bfloat16
    )
    errors_low = jnp.dot(out_grads, full_out, preferred_element_type=jnp.float32).astype(
        jnp.bfloat16
    )
    rows_here = inputs_low.shape[0]
    width = inputs_low.shape[1]
    pieces = owner_dp.shape[1]
    member = piece_of[0][:, None] == jnp.arange(pieces, dtype=jnp.int32)[None, :]
    spread = (member.astype(jnp.bfloat16)[:, :, None] * inputs_low[:, None, :]).reshape(
        rows_here, pieces * width
    )
    partial_value = lax.dot_general(
        spread, errors_low, (((0,), (0,)), ((), ())), preferred_element_type=jnp.float32
    )
    partial_value = partial_value.reshape(pieces, width * width)
    target = owner_dp[0]
    earlier = jnp.arange(pieces)[None, :] < jnp.arange(pieces)[:, None]
    ranked = jnp.sum(((target[:, None] == target[None, :]) & earlier).astype(jnp.int32), axis=1)
    places = target * CAP + ranked
    slots_total = count_dp * CAP
    routing_mask = places[None, :] == jnp.arange(slots_total, dtype=jnp.int32)[:, None]
    outgoing = jnp.dot(
        routing_mask.astype(jnp.float32), partial_value, precision=lax.Precision.HIGHEST
    )
    labels = jnp.sum(routing_mask.astype(jnp.int32) * (owner_slot[0][None, :] + 1), axis=1) - 1
    incoming, arrived = (
        lax.all_to_all(outgoing, "dp", split_axis=0, concat_axis=0, tiled=True),
        lax.all_to_all(labels, "dp", split_axis=0, concat_axis=0, tiled=True),
    )
    owned = count_dp // 2
    collect = (arrived[None, :] == jnp.arange(owned, dtype=jnp.int32)[:, None]).astype(jnp.float32)
    features = jnp.dot(collect, incoming, precision=lax.Precision.HIGHEST).astype(jnp.bfloat16)
    local_gram = lax.dot_general(
        features[:, :GR], features, (((0,), (0,)), ((), ())), preferred_element_type=jnp.float32
    )
    scale_factor = 1.0 / math.sqrt(owned * count_dp * count_fsdp)
    section_one = lax.psum_scatter(local_gram, "fsdp", scatter_dimension=1, tiled=True)
    result = lax.psum_scatter(section_one, "dp", scatter_dimension=0, tiled=True)
    return result * scale_factor


def solution(mesh):
    return jax.shard_map(
        on_device,
        mesh=mesh,
        in_specs=(
            P(("dp", "fsdp"), None),
            P(("dp", "fsdp"), None),
            P(("dp", "fsdp"), None),
            P(("dp", "fsdp"), None),
            P(("dp", "fsdp"), None),
            P("fsdp", None),
            P("fsdp", None),
        ),
        out_specs=P("dp", "fsdp"),
        check_vma=False,
    )
```

profile of v0, /device:TPU:2, one launch (start us, length us, event | category | flops | bytes accessed | tf_op | source)
XLA Modules:
  0.0 862.3 jit_solution(5337309752098964503)
XLA Ops:
  6.5 0.7 all-gather.2.cloned.1.call-update
  7.3 0.9 convert_reduce_fusion
  8.2 0.7 add_bitcast_fusion
  8.8 0.7 fusion.10
  9.5 0.1 select_reduce_fusion
  9.6 0.7 sub.7
  10.3 18.1 %all-to-all-start = ((s32[48,2,1]{1,2,0:T(1,128)}), s32[48,2,1]{1,2,0:T(1,128)S(1)}, u32[]{:S(2)}, u32[]{:S(2)}) async-start(s32[48,2,1]{1,2,0:T(1,128)} %bitcast.4), calls=%async_computation | async-start | bytes 49152 | tf_op jit(solution)/shard_map/all_to_all | solution.py:48
  28.4 0.7 fusion.6
  29.1 47.2 %all_gather.7 = bf16[4096,64]{0,1:T(8,128)(2,1)} all-gather(bf16[256,64]{0,1:T(8,128)(2,1)} %param.13), channel_id=1, replica_groups=mesh['dp'=48,'fsdp'=16] {'fsdp'}, dimensions={0}, use_global_device_ids=true | all-gather | bytes 557056 | tf_op jit(solution)/shard_map/all_gather | solution.py:17
  76.2 25.7 %all-gather.2.cloned.1.call-done = bf16[14336,64]{0,1:T(8,128)(2,1)} async-done(((bf16[896,64]{0,1:T(8,128)(2,1)}), bf16[14336,64]{0,1:T(8,128)(2,1)}) %all-gather.2.cloned.1.call-update) | async-done | bytes 1835024 | tf_op jit(solution)/shard_map/all_gather | solution.py:16
  102.0 4.0 convolution_convert_fusion.2
  106.0 0.1 broadcast_multiply_fusion
  106.0 2.2 fusion
  108.2 0.5 reshape.72
  108.7 0.8 fusion.1
  109.6 2.4 copy.16
  111.9 8.5 all-to-all-start.1
  120.4 0.0 reduce-scatter.2.cloned.1.call-start
  120.5 0.5 broadcast.57
  121.0 0.7 reduce.3
  121.7 0.1 eq.89
  121.8 59.0 %all-to-all-done.1 = f32[48,2,4096]{2,1,0:T(2,128)S(1)} async-done(((f32[48,2,4096]{2,1,0:T(2,128)}), f32[48,2,4096]{2,1,0:T(2,128)S(1)}, u32[]{:S(2)}, u32[]{:S(2)}) %all-to-all-start.1) | async-done | bytes 1572896 | tf_op jit(solution)/shard_map/all_to_all | solution.py:47
  180.8 2.2 all_to_all.12
  183.1 2.0 convolution_convert_fusion
  185.1 2.3 fusion.7
  187.4 0.0 reduce-scatter.2.cloned.1.call-update
  187.4 0.0 all-reduce.3.cloned.1.call-start
  187.4 120.5 %reduce-scatter.2.cloned.1.call-done = f32[192,256]{1,0:T(8,128)} async-done(((f32[192,4096]{1,0:T(8,128)}), f32[192,256]{1,0:T(8,128)}) %reduce-scatter.2.cloned.1.call-update) | async-done | bytes 196624 | tf_op jit(solution)/shard_map/reduce_scatter | solution.py:57
  307.9 0.0 all-reduce.3.cloned.1.call-update
  307.9 1.3 dynamic-slice
  309.9 544.6 %all-reduce.3.cloned.1.call-done = f32[192,256]{1,0:T(8,128)} async-done(((f32[192,256]{1,0:T(8,128)}), f32[192,256]{1,0:T(8,128)}) %all-reduce.3.cloned.1.call-update) | async-done | bytes 196624
  854.5 1.3 dynamic-slice_multiply_fusion
  (6 shorter events, 0.0 us)
Async XLA Ops:
  6.5 99.5 %copy-start = (bf16[128,4096]{1,0:T(8,128)(2,1)S(1)}, bf16[128,4096]{1,0:T(8,128)(2,1)}, u32[]{:S(2)}) copy-start(bf16[128,4096]{1,0:T(8,128)(2,1)} %param.8) | copy-start | bytes 3145732
  6.5 95.4 %all-gather.2.cloned.1.call-start = ((), (), s32[]{:S(2)}) async-start(), calls=%async_computation.3 | async-start | bytes 1949696 | tf_op jit(solution)/shard_map/all_gather | solution.py:16
  10.3 101.6 %all-to-all-start = ((s32[48,2,1]{1,2,0:T(1,128)}), s32[48,2,1]{1,2,0:T(1,128)S(1)}, u32[]{:S(2)}, u32[]{:S(2)}) async-start(s32[48,2,1]{1,2,0:T(1,128)} %bitcast.4), calls=%async_computation | async-start | bytes 49152 | tf_op jit(solution)/shard_map/all_to_all | solution.py:48
  111.9 68.9 %all-to-all-start.1 = ((f32[48,2,4096]{2,1,0:T(2,128)}), f32[48,2,4096]{2,1,0:T(2,128)S(1)}, u32[]{:S(2)}, u32[]{:S(2)}) async-start(f32[48,2,4096]{2,1,0:T(2,128)} %copy.16), calls=%async_computation.1 | async-start | bytes 3145728 | tf_op jit(solution)/shard_map/all_to_all | solution.py:47
  120.4 187.5 %reduce-scatter.2.cloned.1.call-start = ((), (), s32[]{:S(2)}) async-start(), calls=%async_computation.4 | async-start | bytes 3342336 | tf_op jit(solution)/shard_map/reduce_scatter | solution.py:57
  187.4 667.1 %all-reduce.3.cloned.1.call-start = ((), (), s32[]{:S(2)}) async-start(), calls=%async_computation.5 | async-start | bytes 393216
Sparse Core Ops, SparseCore 0:
  11.3 90.6 all-gather.1
  187.5 120.3 reduce-scatter.1
  311.1 543.3 all-reduce.2
where the time goes:
time: 863 us; the launch traced here: 862 us
  waiting for transfers between devices  751 us (87%)
  blocking collectives  47.2 us (5%)
  starting transfers between devices  26.6 us (3%)
  between operations  13.8 us (2%)
  matrix products  11.3 us (1%)
    unnamed x4, waiting for transfers between devices  545 us
    reduce_scatter x1, waiting for transfers between devices, on_device(): lax.psum_scatter(local_gram, 'fsdp', scatter_dimension=1, tiled=True)  120 us
    all_to_all x1, waiting for transfers between devices, on_device(): lax.all_to_all(outgoing, 'dp', split_axis=0, concat_axis=0, tiled=True)  59 us
    all_gather x1, blocking collectives, on_device(): lax.all_gather(sketch_out, 'fsdp', axis=0, tiled=True)  47.2 us
    all_gather x1, waiting for transfers between devices, on_device(): lax.all_gather(sketch_in, 'fsdp', axis=0, tiled=True)  25.7 us
    all_to_all x1, starting transfers between devices, on_device(): lax.all_to_all(labels, 'dp', split_axis=0, concat_axis=0, tiled=True)  18.1 us
  transfers between devices with their start and end apart: 5, of which 4 were waited for; matrix products, arithmetic and copies ran while one was open for 2% of the time, Pallas kernels for 0%

commit v1 on v0

v1 whole, which is shorter than its diff:
```python
import math

import jax
import jax.numpy as jnp
from jax import lax
from jax.sharding import PartitionSpec as P

CAP = 2
GR = 192
SPAN = 5
ROWS = 16


def pack_rows(factors, piece_of, target, slot):
    tokens = factors.shape[0]
    pieces = target.shape[0]
    count_dp = lax.axis_size("dp")
    number = jnp.arange(pieces, dtype=jnp.int32)
    member = piece_of[:, None] == number[None, :]
    first = jnp.sum((piece_of[:, None] < number[None, :]).astype(jnp.int32), axis=0)
    earlier = number[None, :] < number[:, None]
    ranked = jnp.sum(((target[:, None] == target[None, :]) & earlier).astype(jnp.int32), axis=1)
    base = target * ROWS + ranked * SPAN - first
    place = jnp.arange(tokens, dtype=jnp.int32) + jnp.sum(jnp.where(member, base[None, :], 0), axis=1)
    label_place = target * ROWS + CAP * SPAN + ranked
    every = jnp.arange(count_dp * ROWS, dtype=jnp.int32)[:, None]
    select = jnp.concatenate([every == place[None, :], every == label_place[None, :]], axis=1).astype(jnp.bfloat16)
    label_rows = jnp.broadcast_to((slot + 1).astype(jnp.bfloat16)[:, None], (pieces, factors.shape[1]))
    values = jnp.concatenate([factors, label_rows], axis=0)
    packed = jnp.dot(select, values, preferred_element_type=jnp.float32).astype(jnp.bfloat16)
    return packed.reshape(count_dp, ROWS, factors.shape[1])


def on_device(hidden_in, out_grads, piece_of, owner_dp, owner_slot, sketch_in, sketch_out):
    count_dp = lax.axis_size("dp")
    count_fsdp = lax.axis_size("fsdp")
    width = sketch_in.shape[1]
    owned = count_dp // 2
    full_in = lax.all_gather(sketch_in, "fsdp", axis=0, tiled=True)
    full_out = lax.all_gather(sketch_out, "fsdp", axis=0, tiled=True)
    inputs_low = jnp.dot(hidden_in, full_in, preferred_element_type=jnp.float32).astype(jnp.bfloat16)
    errors_low = jnp.dot(out_grads, full_out, preferred_element_type=jnp.float32).astype(jnp.bfloat16)
    factors = jnp.concatenate([inputs_low, errors_low], axis=1)
    packed = pack_rows(factors, piece_of[0], owner_dp[0], owner_slot[0])
    got = lax.all_to_all(packed, "dp", split_axis=0, concat_axis=0, tiled=True)
    labels = got[:, CAP * SPAN : CAP * SPAN + CAP, 0].astype(jnp.int32)
    labels = jnp.repeat(labels, SPAN, axis=1)
    rows = got[:, : CAP * SPAN].reshape(count_dp * CAP * SPAN, 2 * width)
    hit = (labels.reshape(-1)[:, None] == 1 + jnp.arange(owned, dtype=jnp.int32)[None, :]).astype(jnp.bfloat16)
    spread = rows[:, :width][:, :, None] * hit[:, None, :]
    spread = spread.reshape(rows.shape[0], width * owned)
    features = lax.dot_general(spread, rows[:, width:], (((0,), (0,)), ((), ())), preferred_element_type=jnp.float32)
    features = features.astype(jnp.bfloat16)
    share = width // count_fsdp
    head = GR // width
    blocks = features.reshape(count_fsdp, share * owned, width)
    first = jnp.broadcast_to(features[: head * owned][None], (count_fsdp, head * owned, width))
    outgoing = jnp.concatenate([blocks, first], axis=1)
    mixed = lax.all_to_all(outgoing, "fsdp", split_axis=0, concat_axis=0, tiled=True)
    mixed = mixed.reshape(count_fsdp, share + head, owned, width)
    right = mixed[:, :share].transpose(0, 2, 1, 3).reshape(count_fsdp * owned, share * width)
    left = mixed[:, share:].transpose(0, 2, 1, 3).reshape(count_fsdp * owned, head * width)
    local_gram = lax.dot_general(left, right, (((0,), (0,)), ((), ())), preferred_element_type=jnp.float32)
    terms = lax.all_to_all(
        local_gram.reshape(count_dp, GR // count_dp, share * width), "dp", split_axis=0, concat_axis=0, tiled=True
    )
    scale_factor = 1.0 / math.sqrt(owned * count_dp * count_fsdp)
    return jnp.sum(terms, axis=0) * scale_factor


def solution(mesh):
    return jax.shard_map(
        on_device,
        mesh=mesh,
        in_specs=(
            P(("dp", "fsdp"), None),
            P(("dp", "fsdp"), None),
            P(("dp", "fsdp"), None),
            P(("dp", "fsdp"), None),
            P(("dp", "fsdp"), None),
            P("fsdp", None),
            P("fsdp", None),
        ),
        out_specs=P("dp", "fsdp"),
        check_vma=False,
    )
```

time: 863 us -> 201 us (0.23)
  the two profiles are of different devices: /device:TPU:2 before, /device:TPU:1 now
where the time goes in v1:
time: 201 us; the launch traced here: 199 us
  blocking collectives  109 us (54%)
  waiting for transfers between devices  54.7 us (27%)
  between operations  13.6 us (7%)
  starting transfers between devices  7.8 us (4%)
  matrix products  6.32 us (3%)
  other arithmetic  5.01 us (2%)
  local copies, waits for them, and re-layouts  2.61 us (1%)
    all_gather x1, blocking collectives, on_device(): full_out = lax.all_gather(sketch_out, 'fsdp', axis=0, tiled=True)  53.1 us
    all_gather x1, waiting for transfers between devices, on_device(): full_in = lax.all_gather(sketch_in, 'fsdp', axis=0, tiled=True)  40.9 us
    all_to_all x1, blocking collectives, on_device(): lax.all_to_all(outgoing, 'fsdp', split_axis=0, concat_axis=0, tiled=True)  34.5 us
    all_to_all x1, blocking collectives, on_device(): lax.all_to_all(local_gram.reshape(count_dp, GR // count_dp, share * width...  21.8 us
    all_to_all x1, waiting for transfers between devices, on_device(): got = lax.all_to_all(packed, 'dp', split_axis=0, concat_axis=0, tiled=True)  13.1 us
    all_to_all x1, starting transfers between devices, on_device(): got = lax.all_to_all(packed, 'dp', split_axis=0, concat_axis=0, tiled=True)  7.8 us
  transfers between devices with their start and end apart: 2, of which 2 were waited for; matrix products, arithmetic and copies ran while one was open for 2% of the time, Pallas kernels for 0%

profile of v1, /device:TPU:1, one launch (start us, length us, event | category | flops | bytes accessed | tf_op | source)
XLA Modules:
  0.0 199.4 jit_solution(12193202168566483295)
XLA Ops:
  6.5 0.7 all-gather.2.cloned.1.call-update
  7.3 0.7 convert_bitcast_fusion
  7.9 0.8 convert_reduce_fusion
  8.7 0.9 convert_reduce_fusion.1
  9.6 0.7 fusion.12
  10.3 0.7 select_reduce_fusion
  11.2 53.1 %all_gather.7 = bf16[4096,64]{0,1:T(8,128)(2,1)S(1)} all-gather(bf16[256,64]{0,1:T(8,128)(2,1)} %param.13), channel_id=1, replica_groups=mesh['dp'=48,'fsdp'=16] {'fsdp'}, dimensions={0}, use_global_device_ids=true | all-gather | bytes 557056 | tf_op jit(solution)/shard_map/all_gather | solution.py:40
  64.3 0.5 convolution_convert_fusion.2
  64.8 40.9 %all-gather.2.cloned.1.call-done = bf16[14336,64]{0,1:T(8,128)(2,1)} async-done(((bf16[896,64]{0,1:T(8,128)(2,1)}), bf16[14336,64]{0,1:T(8,128)(2,1)}) %all-gather.2.cloned.1.call-update) | async-done | bytes 1835024 | tf_op jit(solution)/shard_map/all_gather | solution.py:39
  105.7 4.0 %convolution_convert_fusion.3 = bf16[128,64]{0,1:T(8,128)(2,1)S(1)} fusion(bf16[128,14336]{1,0:T(8,128)(2,1)} %param.7, bf16[14336,64]{0,1:T(8,128)(2,1)} %all-gather.2.cloned.1.call-done), kind=kOutput, calls=%fused_computation.3 | convolution fusion | flops 234889216 | bytes 5521408 | tf_op jit(solution)/shard_map/dot_general | solution.py:41
  109.7 1.0 convolution_convert_fusion.1
  110.7 7.8 %all-to-all-start = ((bf16[48,16,128]{2,1,0:T(8,128)(2,1)}), bf16[48,16,128]{2,1,0:T(8,128)(2,1)S(1)}, u32[]{:S(2)}, u32[]{:S(2)}) async-start(bf16[48,16,128]{2,1,0:T(8,128)(2,1)} %bitcast.7), calls=%async_computation | async-start | bytes 393216 | tf_op jit(solution)/shard_map/all_to_all | solution.py:45
  118.5 13.1 %all-to-all-done = bf16[48,16,128]{2,1,0:T(8,128)(2,1)S(1)} async-done(((bf16[48,16,128]{2,1,0:T(8,128)(2,1)}), bf16[48,16,128]{2,1,0:T(8,128)(2,1)S(1)}, u32[]{:S(2)}, u32[]{:S(2)}) %all-to-all-start) | async-done | bytes 196640 | tf_op jit(solution)/shard_map/all_to_all | solution.py:45
  131.6 0.1 copy.51
  131.8 0.1 broadcast_in_dim.24
  131.9 0.2 eq.95
  132.2 0.1 copy.41
  132.4 0.1 broadcast_multiply_fusion
  132.5 0.7 convolution_convert_fusion
  133.2 0.2 reshape.88
  133.5 0.2 pad_maximum_fusion
  133.8 34.5 %all_to_all.15 = bf16[16,168,64]{1,2,0:T(8,128)(2,1)S(1)} all-to-all(bf16[16,168,64]{1,2,0:T(8,128)(2,1)S(1)} %pad_maximum_fusion), channel_id=1, replica_groups=mesh['dp'=48,'fsdp'=16] {'fsdp'}, dimensions={0} | all-to-all | bytes 688128 | tf_op jit(solution)/shard_map/all_to_all | solution.py:59
  168.3 0.4 copy.45
  168.7 0.2 copy.48
  168.9 0.3 reshape.93
  169.2 0.2 copy.46
  169.3 0.2 reshape.90
  169.6 0.1 copy.47
  169.8 0.2 fusion.3
  170.0 0.1 copy.50
  170.1 21.8 %all_to_all.16 = f32[48,4,256]{2,1,0:T(4,128)S(1)} all-to-all(f32[48,4,256]{2,1,0:T(4,128)S(1)} %copy.50), channel_id=1, replica_groups=mesh['dp'=48,'fsdp'=16] {'dp'}, dimensions={0} | all-to-all | bytes 393216 | tf_op jit(solution)/shard_map/all_to_all | solution.py:64
  192.0 0.6 broadcast_multiply_fusion.1
  (20 shorter events, 0.7 us)
Async XLA Ops:
  6.5 57.8 %copy-start = (bf16[128,4096]{1,0:T(8,128)(2,1)S(1)}, bf16[128,4096]{1,0:T(8,128)(2,1)}, u32[]{:S(2)}) copy-start(bf16[128,4096]{1,0:T(8,128)(2,1)} %param.8) | copy-start | bytes 3145732
  6.5 99.2 %all-gather.2.cloned.1.call-start = ((), (), s32[]{:S(2)}) async-start(), calls=%async_computation.3 | async-start | bytes 1949696 | tf_op jit(solution)/shard_map/all_gather | solution.py:39
  110.7 20.9 %all-to-all-start = ((bf16[48,16,128]{2,1,0:T(8,128)(2,1)}), bf16[48,16,128]{2,1,0:T(8,128)(2,1)S(1)}, u32[]{:S(2)}, u32[]{:S(2)}) async-start(bf16[48,16,128]{2,1,0:T(8,128)(2,1)} %bitcast.7), calls=%async_computation | async-start | bytes 393216 | tf_op jit(solution)/shard_map/all_to_all | solution.py:45
Sparse Core Ops, SparseCore 0:
  11.3 94.4 all-gather.1

commit v2 on v1

--- a/solution.py
+++ b/solution.py
@@ -3,12 +3,192 @@
 import jax
 import jax.numpy as jnp
 from jax import lax
+from jax.experimental import pallas as pl
+from jax.experimental.pallas import tpu as pltpu
 from jax.sharding import PartitionSpec as P
 
 CAP = 2
 GR = 192
 SPAN = 5
 ROWS = 16
+NX, NY, NZ = 4, 8, 6
+PARTS = 4
+MESH = pl.DeviceIdType.MESH
+
+
+def project_kernel(
+    hidden_hbm, grads_hbm, in_hbm, out_hbm, low_ref,
+    hidden, grads, held, acc_in, acc_out, load_sem, recv_sem, send_sem, edge_sem, inner_sem,
+):
+    d, f = lax.axis_index("dp"), lax.axis_index("fsdp")
+    p, y = d // NY, d % NY
+    x, h, c = f // 4, (f // 2) % 2, f % 2
+    wide_in, wide_out = in_hbm.shape[1], out_hbm.shape[1]
+    step_rows = held.shape[1] // PARTS
+
+    def name(x_, h_, c_):
+        return x_ * 4 + h_ * 2 + c_
+
+    east, west, far = (x + 1) % NX, (x + 3) % NX, (x + 2) % NX
+    up_p, down_p = (p + 1) % NZ, (p + NZ - 1) % NZ
+    up_h, down_h = (h + (p + 1) // NZ) % 2, (h + 1 - (p + NZ - 1) // NZ) % 2
+    to_east, to_west, to_twin = (d, name(east, h, c)), (d, name(west, h, c)), (d, name(x, h, 1 - c))
+    to_up = (up_p * NY + y, name(x, up_h, c))
+    to_down = (down_p * NY + y, name(x, down_h, c))
+    half = p // 3
+    depth = p + half * (5 - 2 * p)
+    to_inner = tuple((1 - half) * a + half * b for a, b in zip(to_up, to_down))
+    to_outer = tuple((1 - half) * b + half * a for a, b in zip(to_up, to_down))
+
+    barrier = pltpu.get_barrier_semaphore()
+    for peer in (to_east, to_west, to_twin, to_up, to_down):
+        pl.semaphore_signal(barrier, inc=1, device_id=peer, device_id_type=MESH)
+
+    loads = (
+        pltpu.make_async_copy(in_hbm, held.at[f, :, pl.ds(0, wide_in)], load_sem.at[0]),
+        pltpu.make_async_copy(out_hbm, held.at[f, :, pl.ds(wide_in, wide_out)], load_sem.at[1]),
+        pltpu.make_async_copy(grads_hbm, grads, load_sem.at[2]),
+        pltpu.make_async_copy(hidden_hbm, hidden, load_sem.at[3]),
+    )
+    for load in loads:
+        load.start()
+
+    def move(shard, part, peer, sem):
+        piece = held.at[shard, pl.ds(pl.multiple_of(part * step_rows, step_rows), step_rows), :]
+        return pltpu.make_async_remote_copy(
+            src_ref=piece, dst_ref=piece, send_sem=sem, recv_sem=recv_sem.at[shard, part],
+            device_id=peer, device_id_type=MESH,
+        )
+
+    def send(shard, part, *peers):
+        for peer in peers:
+            move(shard, part, peer, send_sem).start()
+
+    def arrived(shard, part):
+        move(shard, part, to_twin, send_sem).wait_recv()
+
+    pl.semaphore_wait(barrier, 5)
+    loads[0].wait()
+    loads[1].wait()
+
+    for part in range(PARTS):
+
+        @pl.when(depth == 0)
+        def _():
+            move(f, part, to_outer, edge_sem).start()
+
+        send(f, part, to_east, to_west, to_twin)
+
+    def pass_on(h_, part):
+        for from_x, ahead, goes in ((west, to_east, part < PARTS // 2), (east, to_west, part >= PARTS // 2)):
+            shard = name(from_x, h_, c)
+            arrived(shard, part)
+            if isinstance(goes, bool):
+                if goes:
+                    send(shard, part, ahead)
+            else:
+                pl.when(goes)(lambda: send(shard, part, ahead))
+            send(shard, part, to_twin)
+
+    across = name(x, 1 - h, c)
+
+    @pl.loop(0, 2 * PARTS)
+    def _(t):
+        @pl.when(t < PARTS)
+        def _():
+            pass_on(h, t)
+
+        part = t - 2 * depth
+
+        @pl.when(jnp.logical_and(part >= 0, part < PARTS))
+        def _():
+            arrived(across, part)
+
+            @pl.when(depth < 2)
+            def _():
+                move(across, part, to_inner, inner_sem).start()
+
+            send(across, part, to_east, to_west, to_twin)
+
+    acc_in[...] = jnp.zeros_like(acc_in)
+    acc_out[...] = jnp.zeros_like(acc_out)
+    nt = (((1,), (1,)), ((), ()))
+
+    def use(shard):
+        a = hidden[:, pl.ds(pl.multiple_of(shard * wide_in, 128), wide_in)]
+        acc_in[...] += lax.dot_general(a, held[shard, :, :wide_in], nt, preferred_element_type=jnp.float32)
+        b = grads[:, pl.ds(pl.multiple_of(shard * wide_out, 128), wide_out)]
+        acc_out[...] += lax.dot_general(b, held[shard, :, wide_in:], nt, preferred_element_type=jnp.float32)
+
+    def take(shard):
+        for part in range(PARTS):
+            arrived(shard, part)
+        use(shard)
+
+    def relay_far(h_):
+        for part in range(PARTS):
+            arrived(name(far, h_, c), part)
+            send(name(far, h_, c), part, to_twin)
+
+    relay_far(h)
+    for part in range(PARTS):
+        pass_on(1 - h, part)
+    loads[2].wait()
+    loads[3].wait()
+    for x_ in (x, west, east, far):
+        use(name(x_, h, c))
+    for x_ in (x, west, east):
+        use(name(x_, 1 - h, c))
+    relay_far(1 - h)
+    use(name(far, 1 - h, c))
+    for h_ in (h, 1 - h):
+        for x_ in (x, west, east, far):
+            take(name(x_, h_, 1 - c))
+
+    low_ref[:, :64] = acc_in[...].astype(low_ref.dtype)
+    low_ref[:, 64:] = acc_out[...].astype(low_ref.dtype)
+
+    def drain(count, sem):
+        whole = held.at[pl.ds(0, count)]
+        pltpu.make_async_copy(whole, whole, sem).wait()
+
+    drain(14, send_sem)
+
+    @pl.when(depth == 0)
+    def _():
+        drain(1, edge_sem)
+
+    @pl.when(depth < 2)
+    def _():
+        drain(1, inner_sem)
+
+
+def project(hidden_in, out_grads, sketch_in, sketch_out):
+    rows = hidden_in.shape[0]
+    count = lax.axis_size("fsdp")
+    width = sketch_in.shape[1]
+    wide = sketch_in.shape[0] + sketch_out.shape[0]
+    anywhere = pl.BlockSpec(memory_space=pl.ANY)
+    return pl.pallas_call(
+        project_kernel,
+        out_shape=jax.ShapeDtypeStruct((rows, 2 * width), jnp.bfloat16),
+        in_specs=[anywhere] * 4,
+        out_specs=pl.BlockSpec(memory_space=pltpu.VMEM),
+        scratch_shapes=[
+            pltpu.VMEM(hidden_in.shape, jnp.bfloat16),
+            pltpu.VMEM(out_grads.shape, jnp.bfloat16),
+            pltpu.VMEM((count, width, wide), jnp.bfloat16),
+            pltpu.VMEM((rows, width), jnp.float32),
+            pltpu.VMEM((rows, width), jnp.float32),
+            pltpu.SemaphoreType.DMA((4,)),
+            pltpu.SemaphoreType.DMA((count, PARTS)),
+            pltpu.SemaphoreType.DMA,
+            pltpu.SemaphoreType.DMA,
+            pltpu.SemaphoreType.DMA,
+        ],
+        compiler_params=pltpu.CompilerParams(collective_id=0, has_side_effects=True),
+        name="project",
+    )(hidden_in, out_grads, sketch_in.T, sketch_out.T)
 
 
 def pack_rows(factors, piece_of, target, slot):
@@ -36,11 +216,7 @@
     count_fsdp = lax.axis_size("fsdp")
     width = sketch_in.shape[1]
     owned = count_dp // 2
-    full_in = lax.all_gather(sketch_in, "fsdp", axis=0, tiled=True)
-    full_out = lax.all_gather(sketch_out, "fsdp", axis=0, tiled=True)
-    inputs_low = jnp.dot(hidden_in, full_in, preferred_element_type=jnp.float32).astype(jnp.bfloat16)
-    errors_low = jnp.dot(out_grads, full_out, preferred_element_type=jnp.float32).astype(jnp.bfloat16)
-    factors = jnp.concatenate([inputs_low, errors_low], axis=1)
+    factors = project(hidden_in, out_grads, sketch_in, sketch_out)
     packed = pack_rows(factors, piece_of[0], owner_dp[0], owner_slot[0])
     got = lax.all_to_all(packed, "dp", split_axis=0, concat_axis=0, tiled=True)
     labels = got[:, CAP * SPAN : CAP * SPAN + CAP, 0].astype(jnp.int32)

time: 201 us -> 126 us (0.63)
  blocking collectives: 109 us -> 56.4 us
  waiting for transfers between devices: 54.7 us -> 13 us
  Pallas kernels: 0 us -> 32.3 us
  between operations: 13.6 us -> 0.19 us
  starting transfers between devices: 7.8 us -> 12.6 us
  matrix products: 6.32 us -> 2.64 us
    all_gather x1 -> x0, blocking collectives: 53.1 us -> none  [on_device(): full_out = lax.all_gather(sketch_out, 'fsdp', axis=0, tiled=True)]
    all_gather x1 -> x0, waiting for transfers between devices: 40.9 us -> none  [on_device(): full_in = lax.all_gather(sketch_in, 'fsdp', axis=0, tiled=True)]
    pallas_call x0 -> x1, Pallas kernels: none -> 32.3 us  [project(): pl.pallas_call(project_kernel, out_shape=jax.ShapeDtypeStruct((rows, 2 *...]
    all_to_all x1, starting transfers between devices: 7.8 us -> 12.6 us  [on_device(): got = lax.all_to_all(packed, 'dp', split_axis=0, concat_axis=0, tiled=True)]
    dot_general x2 -> x0, matrix products: 4.49 us -> none  [the longest x1 3.99 us: on_device(): jnp.dot(hidden_in, full_in, preferred_element_type=jnp.float32)]
    all_to_all x1, blocking collectives: 21.8 us -> 23.8 us  [on_device(): lax.all_to_all(local_gram.reshape(count_dp, GR // count_dp, share * width...]
  transfers between devices with their start and end apart: 2 -> 1, of which waited for: 2 -> 1; matrix products, arithmetic and copies ran while one was open for 2% -> 0% of each run, Pallas kernels for 0% -> 0%
where the time goes in v2:
time: 126 us; the launch traced here: 125 us
  blocking collectives  56.4 us (45%)
  Pallas kernels  32.3 us (26%)
  waiting for transfers between devices  13 us (10%)
  starting transfers between devices  12.6 us (10%)
  other arithmetic  5 us (4%)
  matrix products  2.64 us (2%)
  local copies, waits for them, and re-layouts  2.61 us (2%)
    all_to_all x1, blocking collectives, on_device(): lax.all_to_all(outgoing, 'fsdp', split_axis=0, concat_axis=0, tiled=True)  32.6 us
    pallas_call x1, Pallas kernels, project(): pl.pallas_call(project_kernel, out_shape=jax.ShapeDtypeStruct((rows, 2 *...  32.3 us
    all_to_all x1, blocking collectives, on_device(): lax.all_to_all(local_gram.reshape(count_dp, GR // count_dp, share * width...  23.8 us
    all_to_all x1, waiting for transfers between devices, on_device(): got = lax.all_to_all(packed, 'dp', split_axis=0, concat_axis=0, tiled=True)  13 us
    all_to_all x1, starting transfers between devices, on_device(): got = lax.all_to_all(packed, 'dp', split_axis=0, concat_axis=0, tiled=True)  12.6 us
  transfers between devices with their start and end apart: 1, of which 1 were waited for; matrix products, arithmetic and copies ran while one was open for 0% of the time, Pallas kernels for 0%

profile of v2, /device:TPU:1, one launch (start us, length us, event | category | flops | bytes accessed | tf_op | source)
XLA Modules:
  0.0 124.7 jit_solution(4730658458501759725)
XLA Ops:
  0.0 0.8 convert_reduce_fusion
  0.8 0.7 convert_bitcast_fusion
  1.4 0.9 convert_reduce_fusion.1
  2.3 0.7 fusion.10
  3.0 0.7 select_reduce_fusion
  3.8 0.1 iota_compare_fusion.1
  3.9 32.3 %project.1 = bf16[128,128]{1,0:T(8,128)(2,1)} custom-call(bf16[128,14336]{1,0:T(8,128)(2,1)} %hidden_hbm.1, bf16[128,4096]{1,0:T(8,128)(2,1)} %grads_hbm.1, bf16[64,896]{1,0:T(8,128)(2,1)} %bitcast.46, bf16[64,256]{1,0:T(8,128)(2,1)} %bitcast.47), custom_call_target="tpu_custom_call" | custom-call | tf_op jit(solution)/shard_map/project/pallas_call | solution.py:172
  36.2 1.8 %convolution_convert_fusion.1 = bf16[768,128]{1,0:T(8,128)(2,1)} fusion(pred[768,48]{1,0:T(32,128)(4,1)S(1)} %iota_compare_fusion, pred[768,128]{1,0:T(32,128)(4,1)S(1)} %iota_compare_fusion.1, bf16[128,128]{1,0:T(8,128)(2,1)} %project.1, bf16[176]{0:T(256)(128)(2,1)S(1)} %pad.3.clone), kind=kOutput, calls=%fused_computation.1 | convolution fusion | flops 34926592 | bytes 364896 | tf_op jit(solution)/shard_map/dot_general | solution.py:210
  38.0 12.6 %all-to-all-start = ((bf16[48,16,128]{2,1,0:T(8,128)(2,1)}), bf16[48,16,128]{2,1,0:T(8,128)(2,1)S(1)}, u32[]{:S(2)}, u32[]{:S(2)}) async-start(bf16[48,16,128]{2,1,0:T(8,128)(2,1)} %bitcast.9), calls=%async_computation | async-start | bytes 393216 | tf_op jit(solution)/shard_map/all_to_all | solution.py:221
  50.6 13.0 %all-to-all-done = bf16[48,16,128]{2,1,0:T(8,128)(2,1)S(1)} async-done(((bf16[48,16,128]{2,1,0:T(8,128)(2,1)}), bf16[48,16,128]{2,1,0:T(8,128)(2,1)S(1)}, u32[]{:S(2)}, u32[]{:S(2)}) %all-to-all-start) | async-done | bytes 196640 | tf_op jit(solution)/shard_map/all_to_all | solution.py:221
  63.6 0.1 copy.51
  63.7 0.1 copy.43
  63.8 0.1 broadcast_in_dim.24
  64.0 0.2 eq.95
  64.2 0.1 copy.41
  64.3 0.1 compare_convert_fusion
  64.4 0.1 broadcast_multiply_fusion
  64.5 0.7 convolution_convert_fusion
  65.2 0.2 reshape.88
  65.4 0.1 copy.44
  65.5 0.2 pad_maximum_fusion
  65.8 32.6 %all_to_all.15 = bf16[16,168,64]{1,2,0:T(8,128)(2,1)S(1)} all-to-all(bf16[16,168,64]{1,2,0:T(8,128)(2,1)S(1)} %pad_maximum_fusion), channel_id=1, replica_groups=mesh['dp'=48,'fsdp'=16] {'fsdp'}, dimensions={0} | all-to-all | bytes 688128 | tf_op jit(solution)/shard_map/all_to_all | solution.py:235
  98.4 0.4 copy.45
  98.8 0.2 copy.48
  99.0 0.3 reshape.93
  99.3 0.2 copy.46
  99.4 0.2 reshape.90
  99.7 0.1 copy.47
  99.9 0.2 fusion.3
  100.1 0.1 copy.50
  100.2 23.8 %all_to_all.16 = f32[48,4,256]{2,1,0:T(4,128)S(1)} all-to-all(f32[48,4,256]{2,1,0:T(4,128)S(1)} %copy.50), channel_id=1, replica_groups=mesh['dp'=48,'fsdp'=16] {'dp'}, dimensions={0} | all-to-all | bytes 393216 | tf_op jit(solution)/shard_map/all_to_all | solution.py:240
  124.1 0.6 broadcast_multiply_fusion.1
  (13 shorter events, 0.4 us)
Async XLA Ops:
  38.0 25.6 %all-to-all-start = ((bf16[48,16,128]{2,1,0:T(8,128)(2,1)}), bf16[48,16,128]{2,1,0:T(8,128)(2,1)S(1)}, u32[]{:S(2)}, u32[]{:S(2)}) async-start(bf16[48,16,128]{2,1,0:T(8,128)(2,1)} %bitcast.9), calls=%async_computation | async-start | bytes 393216 | tf_op jit(solution)/shard_map/all_to_all | solution.py:221

commit v3 on v2

v3 whole, which is shorter than its diff:
```python
import math

import jax
import jax.numpy as jnp
from jax import lax
from jax.experimental import pallas as pl
from jax.experimental.pallas import tpu as pltpu
from jax.sharding import PartitionSpec as P

CAP = 2
GR = 192
SPAN = 5
ROWS = 16
NX, NY, NZ = 4, 8, 6
ND = NY * NZ
GROUP = 16
EACH = 24
OWN = 24
SHIFT = 12
PARTS = 4
MESH = pl.DeviceIdType.MESH


def iota(shape, axis):
    return lax.broadcasted_iota(jnp.int32, shape, axis).astype(jnp.float32)


def one(mask, dtype=jnp.float32):
    return jnp.where(mask, 1.0, 0.0).astype(dtype)


def place_rows(piece_row, target_row, slot_row, select_ref, label_ref):
    pieces, tokens = target_row.shape[1], piece_row.shape[1]
    square = (pieces, pieces)
    down, along = iota(square, 0), iota(square, 1)
    diagonal = down == along

    def stand(row):
        return jnp.sum(jnp.where(diagonal, row, 0.0), axis=1, keepdims=True)

    target_col, slot_col = stand(target_row), stand(slot_row)
    before = jnp.where(target_col == 0.0, ND - 1.0, target_col - 1.0)
    met = jnp.sum(one(before == target_row), axis=1, keepdims=True)
    first = jnp.max(jnp.where(met == 0.0, target_col, -1.0), axis=0, keepdims=True)

    def order(target):
        ahead = target - first
        return jnp.where(ahead < 0.0, ahead + ND, ahead)

    same = target_col == target_row
    rank_col = jnp.sum(one(same & (along < down)), axis=1, keepdims=True)
    rank_row = jnp.sum(one(same & (down < along)), axis=0, keepdims=True)
    number = iota((pieces, tokens), 0)
    starts = jnp.sum(one(piece_row < number), axis=1, keepdims=True)
    base = order(target_col) * ROWS + rank_col * SPAN - starts
    place = iota((1, tokens), 1) + jnp.sum(jnp.where(piece_row == number, base, 0.0), axis=0, keepdims=True)
    label_place = order(target_row) * ROWS + CAP * SPAN + rank_row
    rows = select_ref.shape[0]
    select_ref[...] = one(iota((rows, tokens), 0) == place, jnp.bfloat16)
    label_at = one(iota((rows, pieces), 0) == label_place, jnp.bfloat16)
    labels = jnp.broadcast_to(slot_col + 1.0, (pieces, label_ref.shape[1])).astype(jnp.bfloat16)
    label_ref[...] = jnp.dot(label_at, labels, preferred_element_type=jnp.float32)


def gram_kernel(
    hidden_hbm, grads_hbm, in_hbm, out_hbm, piece_ref, target_ref, slot_ref, result_ref,
    hidden, grads, held, acc_in, acc_out, select, label_part, turn, spread_label, low, packed, owned_rows,
    feature, mixed, terms, gathered, load_sem, recv_sem, send_sem, edge_sem, inner_sem, swap_send, swap_recv,
):
    d, f = lax.axis_index("dp"), lax.axis_index("fsdp")
    p, y = d // NY, d % NY
    x, h, c = f // 4, (f // 2) % 2, f % 2
    wide_in, wide_out = in_hbm.shape[1], out_hbm.shape[1]
    step_rows = held.shape[1] // PARTS

    def name(x_, h_, c_):
        return x_ * 4 + h_ * 2 + c_

    east, west, far = (x + 1) % NX, (x + 3) % NX, (x + 2) % NX
    up_p, down_p = (p + 1) % NZ, (p + NZ - 1) % NZ
    up_h, down_h = (h + (p + 1) // NZ) % 2, (h + 1 - (p + NZ - 1) // NZ) % 2
    to_east, to_west, to_twin = (d, name(east, h, c)), (d, name(west, h, c)), (d, name(x, h, 1 - c))
    to_up = (up_p * NY + y, name(x, up_h, c))
    to_down = (down_p * NY + y, name(x, down_h, c))
    half = p // 3
    depth = p + half * (5 - 2 * p)
    to_inner = tuple((1 - half) * a + half * b for a, b in zip(to_up, to_down))
    to_outer = tuple((1 - half) * b + half * a for a, b in zip(to_up, to_down))

    def member(other):
        x_, c_ = (x + other // 4) % NX, (c + other % 2) % 2
        y_ = y + ((other // 2) % 2) * (1 - 2 * (y % 2))
        return (p * NY + y_, name(x_, h, c_)), name(x_, y_ % 2, c_)

    def prepare():
        place_rows(
            piece_ref[...].astype(jnp.float32), target_ref[...].astype(jnp.float32),
            slot_ref[...].astype(jnp.float32), select, label_part,
        )
        out_row, lane = iota(turn.shape, 0), iota(turn.shape, 1)
        wanted = jnp.where(out_row < 32.0, 2.0 * out_row, jnp.where(out_row < 64.0, 2.0 * out_row - 63.0, 0.0))
        turn[...] = one(lane == wanted, jnp.bfloat16)
        source = lax.broadcasted_iota(jnp.int32, spread_label.shape, 0)
        goal = lax.broadcasted_iota(jnp.int32, spread_label.shape, 1)
        inside = goal & (ROWS - 1)
        label_row = goal - inside + CAP * SPAN + jnp.where(inside >= SPAN, 1, 0)
        spread_label[...] = one((source == label_row) & (inside < CAP * SPAN), jnp.bfloat16)

    barrier = pltpu.get_barrier_semaphore()

    def greet(peer):
        pl.semaphore_signal(barrier, inc=1, device_id=peer, device_id_type=MESH)

    for peer in (to_east, to_west, to_twin, to_up, to_down):
        greet(peer)
    for other in range(1, GROUP):
        greet(member(other)[0])

    @pl.loop(1, ND)
    def _(j):
        greet(((d + j) % ND, f))
        greet(((d + j) % ND, name(x, 1 - h, c)))

    greet((d, name(x, 1 - h, c)))

    loads = (
        pltpu.make_async_copy(in_hbm, held.at[f, :, pl.ds(0, wide_in)], load_sem.at[0]),
        pltpu.make_async_copy(out_hbm, held.at[f, :, pl.ds(wide_in, wide_out)], load_sem.at[1]),
        pltpu.make_async_copy(grads_hbm, grads, load_sem.at[2]),
        pltpu.make_async_copy(hidden_hbm, hidden, load_sem.at[3]),
    )
    for load in loads:
        load.start()

    def move(shard, part, peer, sem):
        piece = held.at[shard, pl.ds(pl.multiple_of(part * step_rows, step_rows), step_rows), :]
        return pltpu.make_async_remote_copy(
            src_ref=piece, dst_ref=piece, send_sem=sem, recv_sem=recv_sem.at[shard, part],
            device_id=peer, device_id_type=MESH,
        )

    def send(shard, part, *peers):
        for peer in peers:
            move(shard, part, peer, send_sem).start()

    def arrived(shard, part):
        move(shard, part, to_twin, send_sem).wait_recv()

    prepare()
    pl.semaphore_wait(barrier, 5 + (GROUP - 1) + 2 * (ND - 1) + 1)
    loads[0].wait()
    loads[1].wait()

    for part in range(PARTS):

        @pl.when(depth == 0)
        def _():
            move(f, part, to_outer, edge_sem).start()

        send(f, part, to_east, to_west, to_twin)

    def pass_on(h_, part):
        for from_x, ahead, goes in ((west, to_east, part < PARTS // 2), (east, to_west, part >= PARTS // 2)):
            shard = name(from_x, h_, c)
            arrived(shard, part)
            if isinstance(goes, bool):
                if goes:
                    send(shard, part, ahead)
            else:
                pl.when(goes)(lambda: send(shard, part, ahead))
            send(shard, part, to_twin)

    across = name(x, 1 - h, c)

    @pl.loop(0, 2 * PARTS)
    def _(t):
        @pl.when(t < PARTS)
        def _():
            pass_on(h, t)

        part = t - 2 * depth

        @pl.when(jnp.logical_and(part >= 0, part < PARTS))
        def _():
            arrived(across, part)

            @pl.when(depth < 2)
            def _():
                move(across, part, to_inner, inner_sem).start()

            send(across, part, to_east, to_west, to_twin)

    acc_in[...] = jnp.zeros_like(acc_in)
    acc_out[...] = jnp.zeros_like(acc_out)
    nt = (((1,), (1,)), ((), ()))

    def use(shard):
        a = hidden[:, pl.ds(pl.multiple_of(shard * wide_in, 128), wide_in)]
        acc_in[...] += lax.dot_general(a, held[shard, :, :wide_in], nt, preferred_element_type=jnp.float32)
        b = grads[:, pl.ds(pl.multiple_of(shard * wide_out, 128), wide_out)]
        acc_out[...] += lax.dot_general(b, held[shard, :, wide_in:], nt, preferred_element_type=jnp.float32)

    def take(shard):
        for part in range(PARTS):
            arrived(shard, part)
        use(shard)

    def relay_far(h_):
        for part in range(PARTS):
            arrived(name(far, h_, c), part)
            send(name(far, h_, c), part, to_twin)

    relay_far(h)
    for part in range(PARTS):
        pass_on(1 - h, part)
    loads[2].wait()
    loads[3].wait()
    for x_ in (x, west, east, far):
        use(name(x_, h, c))
    for x_ in (x, west, east):
        use(name(x_, 1 - h, c))
    relay_far(1 - h)
    use(name(far, 1 - h, c))
    for h_ in (h, 1 - h):
        for x_ in (x, west, east, far):
            take(name(x_, h_, 1 - c))

    def drain(ref, count, sem):
        whole = ref.at[pl.ds(0, count)]
        pltpu.make_async_copy(whole, whole, sem).wait()

    low[:, :64] = acc_in[...].astype(low.dtype)
    low[:, 64:] = acc_out[...].astype(low.dtype)
    blocks = jnp.dot(select[...], low[...], preferred_element_type=jnp.float32) + label_part[...]
    packed[...] = blocks.astype(jnp.bfloat16).reshape(packed.shape)

    def post(src, dst, peer, phase):
        pltpu.make_async_remote_copy(
            src_ref=src, dst_ref=dst, send_sem=swap_send.at[phase], recv_sem=swap_recv.at[phase],
            device_id=peer, device_id_type=MESH,
        ).start()

    def keep(src, dst, phase):
        pltpu.make_async_copy(src, dst, swap_recv.at[phase]).start()

    keep(packed.at[SHIFT], owned_rows.at[SHIFT], 0)

    @pl.loop(1, EACH)
    def _(j):
        k = (SHIFT + j) % EACH
        post(packed.at[k], owned_rows.at[k], ((d + k + ND - SHIFT) % ND, f), 0)

    drain(owned_rows, EACH, swap_recv.at[0])

    rows = owned_rows[...].reshape(EACH * ROWS, 128)
    turned = lax.dot_general(turn[...], rows, nt, preferred_element_type=jnp.float32)
    label_rows = jnp.dot(turned[64:80].astype(jnp.bfloat16), spread_label[...], preferred_element_type=jnp.float32)
    hit = one(label_rows[:1] == iota((OWN, EACH * ROWS), 0) + 1.0)
    high = iota(rows.shape, 1) >= 64.0
    rows32 = rows.astype(jnp.float32)
    value_odd = jnp.where(high, rows32, 0.0).astype(jnp.bfloat16)
    value_even = jnp.where(high, 0.0, pltpu.roll(rows32, 64, 1)).astype(jnp.bfloat16)

    def expand(block):
        wide = block[:, None, :] * hit[None]
        return wide.reshape(32 * OWN, EACH * ROWS).astype(jnp.bfloat16)

    made = jnp.dot(expand(turned[:32]), value_even, preferred_element_type=jnp.float32)
    made += jnp.dot(expand(turned[32:64]), value_odd, preferred_element_type=jnp.float32)
    feature[...] = made.astype(jnp.bfloat16).reshape(feature.shape)

    here = name(x, y % 2, c)
    keep(feature.at[here], mixed.at[2 * here], 1)
    keep(feature.at[0], mixed.at[2 * here + 1], 1)
    for other in range(GROUP - 1, 0, -1):
        peer, columns = member(other)
        post(feature.at[columns], mixed.at[2 * here], peer, 1)
        post(feature.at[0], mixed.at[2 * here + 1], peer, 1)
    drain(mixed, 2 * GROUP, swap_recv.at[1])

    both = mixed[...].astype(jnp.float32).reshape(GROUP, 2, 2, OWN, 128)
    tn = (((0,), (0,)), ((), ()))

    def side(which, pair):
        return both[:, which, pair].reshape(GROUP * OWN, 128).astype(jnp.bfloat16)

    lefts = (side(1, 0), side(1, 1))
    tiles = []
    for pair in range(2):
        right = side(0, pair)
        top = lax.dot_general(lefts[0], right, tn, preferred_element_type=jnp.float32)
        low_part = lax.dot_general(lefts[1], right, tn, preferred_element_type=jnp.float32)
        tiles.append(jnp.concatenate([top, low_part[: GR - 128]], axis=0).reshape(GR // 8, 8, 128))
    upper = lax.broadcasted_iota(jnp.int32, tiles[0].shape, 1) < 4
    terms[:, 0] = jnp.where(upper, tiles[0], pltpu.roll(tiles[1], 4, 1))
    terms[:, 1] = jnp.where(upper, pltpu.roll(tiles[0], 4, 1), tiles[1])

    column = name(x, y % 2, c)
    mine = h * (ND // 2) + p * (NY // 2) + y // 2
    at_home = (y % 2) == h

    def term(o):
        return terms.at[o // 2, o % 2]

    @pl.when(at_home)
    def _():
        keep(term(d), gathered.at[mine], 2)

    @pl.when(jnp.logical_not(at_home))
    def _():
        post(term(d), gathered.at[mine], (d, column), 2)

    @pl.loop(1, ND)
    def _(j):
        o = (d + j) % ND
        post(term(o), gathered.at[mine], (o, column), 2)

    drain(gathered, ND, swap_recv.at[2])
    total = jnp.sum(gathered[...], axis=0) * (1.0 / math.sqrt(OWN * ND * GROUP))
    result_ref[:, :128] = total[:4]
    result_ref[:, 128:] = total[4:]

    drain(held, 14, send_sem)

    @pl.when(depth == 0)
    def _():
        drain(held, 1, edge_sem)

    @pl.when(depth < 2)
    def _():
        drain(held, 1, inner_sem)

    drain(packed, EACH - 1, swap_send.at[0])
    drain(mixed, 2 * (GROUP - 1), swap_send.at[1])

    @pl.when(at_home)
    def _():
        drain(gathered, ND - 1, swap_send.at[2])

    @pl.when(jnp.logical_not(at_home))
    def _():
        drain(gathered, ND, swap_send.at[2])


def on_device(hidden_in, out_grads, piece_of, owner_dp, owner_slot, sketch_in, sketch_out):
    rows = hidden_in.shape[0]
    width = sketch_in.shape[1]
    wide = sketch_in.shape[0] + sketch_out.shape[0]
    anywhere = pl.BlockSpec(memory_space=pl.ANY)
    vmem = pl.BlockSpec(memory_space=pltpu.VMEM)
    bf16, f32 = jnp.bfloat16, jnp.float32
    return pl.pallas_call(
        gram_kernel,
        out_shape=jax.ShapeDtypeStruct((GR // ND, 4096 // GROUP), f32),
        in_specs=[anywhere] * 4 + [vmem] * 3,
        out_specs=vmem,
        scratch_shapes=[
            pltpu.VMEM(hidden_in.shape, bf16),
            pltpu.VMEM(out_grads.shape, bf16),
            pltpu.VMEM((GROUP, width, wide), bf16),
            pltpu.VMEM((rows, width), f32),
            pltpu.VMEM((rows, width), f32),
            pltpu.VMEM((EACH * ROWS, rows), bf16),
            pltpu.VMEM((EACH * ROWS, 128), f32),
            pltpu.VMEM((80, 128), bf16),
            pltpu.VMEM((EACH * ROWS, EACH * ROWS), bf16),
            pltpu.VMEM((rows, 128), bf16),
            pltpu.VMEM((EACH, ROWS, 128), bf16),
            pltpu.VMEM((EACH, ROWS, 128), bf16),
            pltpu.VMEM((GROUP, 2 * OWN, 128), bf16),
            pltpu.VMEM((2 * GROUP, 2 * OWN, 128), bf16),
            pltpu.VMEM((GR // 8, 2, 8, 128), f32),
            pltpu.VMEM((ND, 8, 128), f32),
            pltpu.SemaphoreType.DMA((4,)),
            pltpu.SemaphoreType.DMA((GROUP, PARTS)),
            pltpu.SemaphoreType.DMA,
            pltpu.SemaphoreType.DMA,
            pltpu.SemaphoreType.DMA,
            pltpu.SemaphoreType.DMA((3,)),
            pltpu.SemaphoreType.DMA((3,)),
        ],
        compiler_params=pltpu.CompilerParams(collective_id=0, has_side_effects=True),
        name="gram",
    )(hidden_in, out_grads, sketch_in.T, sketch_out.T, piece_of, owner_dp, owner_slot)


def solution(mesh):
    return jax.shard_map(
        on_device,
        mesh=mesh,
        in_specs=(
            P(("dp", "fsdp"), None),
            P(("dp", "fsdp"), None),
            P(("dp", "fsdp"), None),
            P(("dp", "fsdp"), None),
            P(("dp", "fsdp"), None),
            P("fsdp", None),
            P("fsdp", None),
        ),
        out_specs=P("dp", "fsdp"),
        check_vma=False,
    )
```

time: 126 us -> 74.3 us (0.59)
  the two profiles are of different devices: /device:TPU:1 before, /device:TPU:64 now
where the time goes in v3:
time: 74.3 us; the launch traced here: 74.1 us
  Pallas kernels  72.8 us (98%)
  local copies, waits for them, and re-layouts  1.28 us (2%)
    pallas_call x1, Pallas kernels, on_device(): pl.pallas_call(gram_kernel, out_shape=jax.ShapeDtypeStruct((GR // ND, 409...  72.8 us

profile of v3, /device:TPU:64, one launch (start us, length us, event | category | flops | bytes accessed | tf_op | source)
XLA Modules:
  0.0 74.1 jit_solution(17520723884565292728)
XLA Ops:
  0.0 72.8 %gram.1 = f32[4,256]{1,0:T(4,128)} custom-call(bf16[128,14336]{1,0:T(8,128)(2,1)} %hidden_hbm.1, bf16[128,4096]{1,0:T(8,128)(2,1)} %grads_hbm.1, bf16[64,896]{1,0:T(8,128)(2,1)} %bitcast.2, bf16[64,256]{1,0:T(8,128)(2,1)} %bitcast.3, s32[1,128]{1,0:T(1,128)} %piece_ref.1, s32[1,48]{1,0:T(1,128)} %target_ref.1, s32[1,48]{1,0:T(1,128)} %slot_ref.1), custom_call_target="tpu_custom_call" | custom-call | tf_op jit(solution)/shard_map/gram/pallas_call | solution.py:352
  72.8 1.3 %copy.9 = f32[4,256]{1,0:T(4,128)} copy(f32[4,256]{1,0:T(4,128)} %gram.1) | data formatting | bytes 8192

commit v4 on v3

--- a/solution.py
+++ b/solution.py
@@ -17,6 +17,7 @@
 EACH = 24
 OWN = 24
 SHIFT = 12
+ROUNDS = 7
 PARTS = 4
 MESH = pl.DeviceIdType.MESH
 
@@ -62,26 +63,44 @@
     label_ref[...] = jnp.dot(label_at, labels, preferred_element_type=jnp.float32)
 
 
+def prepare_tables(piece_row, target_row, slot_row, select, label_part, turn, spread_label):
+    place_rows(piece_row, target_row, slot_row, select, label_part)
+    out_row, lane = iota(turn.shape, 0), iota(turn.shape, 1)
+    wanted = jnp.where(out_row < 32.0, 2.0 * out_row, jnp.where(out_row < 64.0, 2.0 * out_row - 63.0, 0.0))
+    turn[...] = one(lane == wanted, jnp.bfloat16)
+    source = lax.broadcasted_iota(jnp.int32, spread_label.shape, 0)
+    goal = lax.broadcasted_iota(jnp.int32, spread_label.shape, 1)
+    inside = goal & (ROWS - 1)
+    label_row = goal - inside + CAP * SPAN + jnp.where(inside >= SPAN, 1, 0)
+    spread_label[...] = one((source == label_row) & (inside < CAP * SPAN), jnp.bfloat16)
+
+
 def gram_kernel(
     hidden_hbm, grads_hbm, in_hbm, out_hbm, piece_ref, target_ref, slot_ref, result_ref,
     hidden, grads, held, acc_in, acc_out, select, label_part, turn, spread_label, low, packed, owned_rows,
-    feature, mixed, terms, gathered, load_sem, recv_sem, send_sem, edge_sem, inner_sem, swap_send, swap_recv,
+    feature, mixed, terms, gathered, load_sem, recv_sem, send_sem, edge_sem, inner_sem, swap_send, swap_recv, round_sem,
 ):
     d, f = lax.axis_index("dp"), lax.axis_index("fsdp")
     p, y = d // NY, d % NY
     x, h, c = f // 4, (f // 2) % 2, f % 2
+    side_y = y % 2
     wide_in, wide_out = in_hbm.shape[1], out_hbm.shape[1]
     step_rows = held.shape[1] // PARTS
 
     def name(x_, h_, c_):
         return x_ * 4 + h_ * 2 + c_
 
+    def along_z(steps):
+        z_ = (h * NZ + p + steps + 2 * NZ) % (2 * NZ)
+        return ((z_ % NZ) * NY + y, name(x, z_ // NZ, c))
+
+    def along_y(steps):
+        return (p * NY + (y + steps + NY) % NY, f)
+
     east, west, far = (x + 1) % NX, (x + 3) % NX, (x + 2) % NX
-    up_p, down_p = (p + 1) % NZ, (p + NZ - 1) % NZ
-    up_h, down_h = (h + (p + 1) // NZ) % 2, (h + 1 - (p + NZ - 1) // NZ) % 2
     to_east, to_west, to_twin = (d, name(east, h, c)), (d, name(west, h, c)), (d, name(x, h, 1 - c))
-    to_up = (up_p * NY + y, name(x, up_h, c))
-    to_down = (down_p * NY + y, name(x, down_h, c))
+    to_up, to_down = along_z(1), along_z(-1)
+    to_pair = (p * NY + y + 1 - 2 * side_y, f)
     half = p // 3
     depth = p + half * (5 - 2 * p)
     to_inner = tuple((1 - half) * a + half * b for a, b in zip(to_up, to_down))
@@ -89,39 +108,12 @@
 
     def member(other):
         x_, c_ = (x + other // 4) % NX, (c + other % 2) % 2
-        y_ = y + ((other // 2) % 2) * (1 - 2 * (y % 2))
-        return (p * NY + y_, name(x_, h, c_)), name(x_, y_ % 2, c_)
-
-    def prepare():
-        place_rows(
-            piece_ref[...].astype(jnp.float32), target_ref[...].astype(jnp.float32),
-            slot_ref[...].astype(jnp.float32), select, label_part,
-        )
-        out_row, lane = iota(turn.shape, 0), iota(turn.shape, 1)
-        wanted = jnp.where(out_row < 32.0, 2.0 * out_row, jnp.where(out_row < 64.0, 2.0 * out_row - 63.0, 0.0))
-        turn[...] = one(lane == wanted, jnp.bfloat16)
-        source = lax.broadcasted_iota(jnp.int32, spread_label.shape, 0)
-        goal = lax.broadcasted_iota(jnp.int32, spread_label.shape, 1)
-        inside = goal & (ROWS - 1)
-        label_row = goal - inside + CAP * SPAN + jnp.where(inside >= SPAN, 1, 0)
-        spread_label[...] = one((source == label_row) & (inside < CAP * SPAN), jnp.bfloat16)
+        y_ = y + ((other // 2) % 2) * (1 - 2 * side_y)
+        return (p * NY + y_, name(x_, h, c_)), name(x_, (y_ + p) % 2, c_)
 
     barrier = pltpu.get_barrier_semaphore()
-
-    def greet(peer):
+    for peer in (to_east, to_west, to_twin, to_up, to_down, along_y(1), along_y(-1)):
         pl.semaphore_signal(barrier, inc=1, device_id=peer, device_id_type=MESH)
-
-    for peer in (to_east, to_west, to_twin, to_up, to_down):
-        greet(peer)
-    for other in range(1, GROUP):
-        greet(member(other)[0])
-
-    @pl.loop(1, ND)
-    def _(j):
-        greet(((d + j) % ND, f))
-        greet(((d + j) % ND, name(x, 1 - h, c)))
-
-    greet((d, name(x, 1 - h, c)))
 
     loads = (
         pltpu.make_async_copy(in_hbm, held.at[f, :, pl.ds(0, wide_in)], load_sem.at[0]),
@@ -132,6 +124,22 @@
     for load in loads:
         load.start()
 
+    circles = (
+        (to_east, to_west, to_twin), (to_twin,), (along_y(1), along_y(-1)), (along_y(2), along_y(-2)),
+        (to_up, to_down), (along_z(2), along_z(-2)), (along_z(3), along_z(-3)),
+    )
+
+    def tell(number):
+        for peer in circles[number]:
+            pl.semaphore_signal(round_sem.at[number], inc=1, device_id=peer, device_id_type=MESH)
+
+    def hear(number):
+        pl.semaphore_wait(round_sem.at[number], len(circles[number]))
+
+    def hear_and_tell(number):
+        hear(number)
+        tell(number + 1)
+
     def move(shard, part, peer, sem):
         piece = held.at[shard, pl.ds(pl.multiple_of(part * step_rows, step_rows), step_rows), :]
         return pltpu.make_async_remote_copy(
@@ -146,53 +154,71 @@
     def arrived(shard, part):
         move(shard, part, to_twin, send_sem).wait_recv()
 
-    prepare()
-    pl.semaphore_wait(barrier, 5 + (GROUP - 1) + 2 * (ND - 1) + 1)
+    def part_of(q):
+        return (q % 2) * 2 + (q // 2) * (1 - 2 * side_y) + side_y
+
+    pl.semaphore_wait(barrier, 7)
     loads[0].wait()
     loads[1].wait()
 
-    for part in range(PARTS):
+    for q in range(PARTS):
 
         @pl.when(depth == 0)
         def _():
-            move(f, part, to_outer, edge_sem).start()
-
-        send(f, part, to_east, to_west, to_twin)
-
-    def pass_on(h_, part):
-        for from_x, ahead, goes in ((west, to_east, part < PARTS // 2), (east, to_west, part >= PARTS // 2)):
-            shard = name(from_x, h_, c)
-            arrived(shard, part)
-            if isinstance(goes, bool):
-                if goes:
-                    send(shard, part, ahead)
-            else:
-                pl.when(goes)(lambda: send(shard, part, ahead))
-            send(shard, part, to_twin)
+            move(f, part_of(q), to_outer, edge_sem).start()
+
+        if q < 3:
+            send(f, part_of(q), to_east, to_west)
+        send(f, part_of(q), to_twin)
+    tell(0)
+
+    def near(h_, q):
+        part = part_of(q)
+        first, second = name(west, h_, c), name(east, h_, c)
+        arrived(first, part)
+        if q == 0:
+            send(first, part, to_east)
+        if q == 1:
+            send(first, part, to_pair)
+        send(first, part, to_twin)
+        arrived(second, part)
+        if q == 1:
+            send(second, part, to_west, to_pair)
+        send(second, part, to_twin)
+
+    def remote(h_, q):
+        shard, part = name(far, h_, c), part_of(q)
+        arrived(shard, part)
+        if q < 2:
+            send(shard, part, to_pair)
+        send(shard, part, to_twin)
 
     across = name(x, 1 - h, c)
 
-    @pl.loop(0, 2 * PARTS)
-    def _(t):
-        @pl.when(t < PARTS)
+    for t in range(2 * PARTS):
+        if t < 3:
+            near(h, t)
+        q = t - 2 * depth
+
+        @pl.when(jnp.logical_and(q >= 0, q < PARTS))
         def _():
-            pass_on(h, t)
-
-        part = t - 2 * depth
-
-        @pl.when(jnp.logical_and(part >= 0, part < PARTS))
-        def _():
+            part = part_of(q)
             arrived(across, part)
 
             @pl.when(depth < 2)
             def _():
                 move(across, part, to_inner, inner_sem).start()
 
-            send(across, part, to_east, to_west, to_twin)
-
-    acc_in[...] = jnp.zeros_like(acc_in)
-    acc_out[...] = jnp.zeros_like(acc_out)
-    nt = (((1,), (1,)), ((), ()))
+            @pl.when(q < 3)
+            def _():
+                send(across, part, to_east, to_west)
+
+            send(across, part, to_twin)
+
+        if t == 3:
+            hear_and_tell(0)
+        if t == 5:
+            hear_and_tell(1)
 
     def use(shard):
         a = hidden[:, pl.ds(pl.multiple_of(shard * wide_in, 128), wide_in)]
@@ -205,25 +231,41 @@
             arrived(shard, part)
         use(shard)
 
-    def relay_far(h_):
-        for part in range(PARTS):
-            arrived(name(far, h_, c), part)
-            send(name(far, h_, c), part, to_twin)
-
-    relay_far(h)
-    for part in range(PARTS):
-        pass_on(1 - h, part)
+    nt = (((1,), (1,)), ((), ()))
+    acc_in[...] = jnp.zeros_like(acc_in)
+    acc_out[...] = jnp.zeros_like(acc_out)
+    remote(h, 0)
+    remote(h, 1)
+    hear_and_tell(2)
+    near(1 - h, 0)
+    near(h, 3)
+    hear_and_tell(3)
+    near(1 - h, 1)
+    remote(h, 2)
+    remote(h, 3)
+    near(1 - h, 2)
+    hear_and_tell(4)
+    remote(1 - h, 0)
+    remote(1 - h, 1)
+    prepare_tables(
+        piece_ref[...].astype(jnp.float32), target_ref[...].astype(jnp.float32), slot_ref[...].astype(jnp.float32),
+        select, label_part, turn, spread_label,
+    )
     loads[2].wait()
     loads[3].wait()
     for x_ in (x, west, east, far):
         use(name(x_, h, c))
-    for x_ in (x, west, east):
+    hear_and_tell(5)
+    near(1 - h, 3)
+    remote(1 - h, 2)
+    remote(1 - h, 3)
+    for x_ in (x, west, east, far):
+        take(name(x_, h, 1 - c))
+    for x_ in (x, west, east, far):
         use(name(x_, 1 - h, c))
-    relay_far(1 - h)
-    use(name(far, 1 - h, c))
-    for h_ in (h, 1 - h):
-        for x_ in (x, west, east, far):
-            take(name(x_, h_, 1 - c))
+    for x_ in (x, west, east, far):
+        take(name(x_, 1 - h, 1 - c))
+    hear(6)
 
     def drain(ref, count, sem):
         whole = ref.at[pl.ds(0, count)]
@@ -269,7 +311,7 @@
     made += jnp.dot(expand(turned[32:64]), value_odd, preferred_element_type=jnp.float32)
     feature[...] = made.astype(jnp.bfloat16).reshape(feature.shape)
 
-    here = name(x, y % 2, c)
+    here = name(x, (y + p) % 2, c)
     keep(feature.at[here], mixed.at[2 * here], 1)
     keep(feature.at[0], mixed.at[2 * here + 1], 1)
     for other in range(GROUP - 1, 0, -1):
@@ -292,12 +334,12 @@
         low_part = lax.dot_general(lefts[1], right, tn, preferred_element_type=jnp.float32)
         tiles.append(jnp.concatenate([top, low_part[: GR - 128]], axis=0).reshape(GR // 8, 8, 128))
     upper = lax.broadcasted_iota(jnp.int32, tiles[0].shape, 1) < 4
-    terms[:, 0] = jnp.where(upper, tiles[0], pltpu.roll(tiles[1], 4, 1))
-    terms[:, 1] = jnp.where(upper, pltpu.roll(tiles[0], 4, 1), tiles[1])
-
-    column = name(x, y % 2, c)
+    terms[:, 0] = jnp.where(upper, tiles[0], pltpu.roll(tiles[1], 4, 1)).astype(terms.dtype)
+    terms[:, 1] = jnp.where(upper, pltpu.roll(tiles[0], 4, 1), tiles[1]).astype(terms.dtype)
+
+    column = name(x, (y + p) % 2, c)
     mine = h * (ND // 2) + p * (NY // 2) + y // 2
-    at_home = (y % 2) == h
+    at_home = ((y + p) % 2) == h
 
     def term(o):
         return terms.at[o // 2, o % 2]
@@ -316,7 +358,7 @@
         post(term(o), gathered.at[mine], (o, column), 2)
 
     drain(gathered, ND, swap_recv.at[2])
-    total = jnp.sum(gathered[...], axis=0) * (1.0 / math.sqrt(OWN * ND * GROUP))
+    total = jnp.sum(gathered[...].astype(jnp.float32), axis=0)
     result_ref[:, :128] = total[:4]
     result_ref[:, 128:] = total[4:]
 
@@ -349,7 +391,7 @@
     anywhere = pl.BlockSpec(memory_space=pl.ANY)
     vmem = pl.BlockSpec(memory_space=pltpu.VMEM)
     bf16, f32 = jnp.bfloat16, jnp.float32
-    return pl.pallas_call(
+    total = pl.pallas_call(
         gram_kernel,
         out_shape=jax.ShapeDtypeStruct((GR // ND, 4096 // GROUP), f32),
         in_specs=[anywhere] * 4 + [vmem] * 3,
@@ -369,8 +411,8 @@
             pltpu.VMEM((EACH, ROWS, 128), bf16),
             pltpu.VMEM((GROUP, 2 * OWN, 128), bf16),
             pltpu.VMEM((2 * GROUP, 2 * OWN, 128), bf16),
-            pltpu.VMEM((GR // 8, 2, 8, 128), f32),
-            pltpu.VMEM((ND, 8, 128), f32),
+            pltpu.VMEM((GR // 8, 2, 8, 128), bf16),
+            pltpu.VMEM((ND, 8, 128), bf16),
             pltpu.SemaphoreType.DMA((4,)),
             pltpu.SemaphoreType.DMA((GROUP, PARTS)),
             pltpu.SemaphoreType.DMA,
@@ -378,10 +420,12 @@
             pltpu.SemaphoreType.DMA,
             pltpu.SemaphoreType.DMA((3,)),
             pltpu.SemaphoreType.DMA((3,)),
+            pltpu.SemaphoreType.REGULAR((ROUNDS,)),
         ],
         compiler_params=pltpu.CompilerParams(collective_id=0, has_side_effects=True),
         name="gram",
     )(hidden_in, out_grads, sketch_in.T, sketch_out.T, piece_of, owner_dp, owner_slot)
+    return total * (1.0 / math.sqrt(OWN * ND * GROUP))
 
 
 def solution(mesh):

time: 74.3 us -> 64.9 us (0.87)
  the two profiles are of different devices: /device:TPU:64 before, /device:TPU:1 now
where the time goes in v4:
time: 64.9 us; the launch traced here: 64.7 us
  Pallas kernels  63.4 us (98%)
  other arithmetic  1.28 us (2%)
    pallas_call x1, Pallas kernels, on_device(): pl.pallas_call(gram_kernel, out_shape=jax.ShapeDtypeStruct((GR // ND, 409...  63.4 us

profile of v4, /device:TPU:1, one launch (start us, length us, event | category | flops | bytes accessed | tf_op | source)
XLA Modules:
  0.0 64.7 jit_solution(17111586937792768390)
XLA Ops:
  0.0 63.4 %gram.1 = f32[4,256]{1,0:T(4,128)} custom-call(bf16[128,14336]{1,0:T(8,128)(2,1)} %hidden_hbm.1, bf16[128,4096]{1,0:T(8,128)(2,1)} %grads_hbm.1, bf16[64,896]{1,0:T(8,128)(2,1)} %bitcast.2, bf16[64,256]{1,0:T(8,128)(2,1)} %bitcast.3, s32[1,128]{1,0:T(1,128)} %piece_ref.1, s32[1,48]{1,0:T(1,128)} %target_ref.1, s32[1,48]{1,0:T(1,128)} %slot_ref.1), custom_call_target="tpu_custom_call" | custom-call | tf_op jit(solution)/shard_map/gram/pallas_call | solution.py:394
  63.4 1.3 %broadcast_multiply_fusion = f32[4,256]{1,0:T(4,128)} fusion(f32[4,256]{1,0:T(4,128)} %gram.1), kind=kLoop, calls=%fused_computation | loop fusion | flops 1024 | bytes 8192 | tf_op jit(solution)/shard_map/mul | solution.py:428

commit v5 on v4

--- a/solution.py
+++ b/solution.py
@@ -76,14 +76,13 @@
 
 
 def gram_kernel(
-    hidden_hbm, grads_hbm, in_hbm, out_hbm, piece_ref, target_ref, slot_ref, result_ref,
-    hidden, grads, held, acc_in, acc_out, select, label_part, turn, spread_label, low, packed, owned_rows,
+    hidden_hbm, grads_hbm, in_hbm, out_hbm, piece_hbm, target_hbm, slot_hbm, result_ref,
+    piece_ref, target_ref, slot_ref, hidden, grads, held, acc_in, acc_out, select, label_part, turn, spread_label, low, packed, owned_rows,
     feature, mixed, terms, gathered, load_sem, recv_sem, send_sem, edge_sem, inner_sem, swap_send, swap_recv, round_sem,
 ):
     d, f = lax.axis_index("dp"), lax.axis_index("fsdp")
     p, y = d // NY, d % NY
     x, h, c = f // 4, (f // 2) % 2, f % 2
-    side_y = y % 2
     wide_in, wide_out = in_hbm.shape[1], out_hbm.shape[1]
     step_rows = held.shape[1] // PARTS
 
@@ -100,7 +99,7 @@
     east, west, far = (x + 1) % NX, (x + 3) % NX, (x + 2) % NX
     to_east, to_west, to_twin = (d, name(east, h, c)), (d, name(west, h, c)), (d, name(x, h, 1 - c))
     to_up, to_down = along_z(1), along_z(-1)
-    to_pair = (p * NY + y + 1 - 2 * side_y, f)
+    to_far = (d, name(far, h, c))
     half = p // 3
     depth = p + half * (5 - 2 * p)
     to_inner = tuple((1 - half) * a + half * b for a, b in zip(to_up, to_down))
@@ -108,11 +107,11 @@
 
     def member(other):
         x_, c_ = (x + other // 4) % NX, (c + other % 2) % 2
-        y_ = y + ((other // 2) % 2) * (1 - 2 * side_y)
+        y_ = y + ((other // 2) % 2) * (1 - 2 * (y % 2))
         return (p * NY + y_, name(x_, h, c_)), name(x_, (y_ + p) % 2, c_)
 
     barrier = pltpu.get_barrier_semaphore()
-    for peer in (to_east, to_west, to_twin, to_up, to_down, along_y(1), along_y(-1)):
+    for peer in (to_east, to_west, to_far, to_twin, to_up, to_down, along_y(1), along_y(-1)):
         pl.semaphore_signal(barrier, inc=1, device_id=peer, device_id_type=MESH)
 
     loads = (
@@ -120,9 +119,10 @@
         pltpu.make_async_copy(out_hbm, held.at[f, :, pl.ds(wide_in, wide_out)], load_sem.at[1]),
         pltpu.make_async_copy(grads_hbm, grads, load_sem.at[2]),
         pltpu.make_async_copy(hidden_hbm, hidden, load_sem.at[3]),
+        pltpu.make_async_copy(piece_hbm, piece_ref, load_sem.at[4]),
+        pltpu.make_async_copy(target_hbm, target_ref, load_sem.at[5]),
+        pltpu.make_async_copy(slot_hbm, slot_ref, load_sem.at[6]),
     )
-    for load in loads:
-        load.start()
 
     circles = (
         (to_east, to_west, to_twin), (to_twin,), (along_y(1), along_y(-1)), (along_y(2), along_y(-2)),
@@ -151,74 +151,62 @@
         for peer in peers:
             move(shard, part, peer, send_sem).start()
 
+    def first_send(part, peer, sem):
+        rows_ = pl.ds(part * step_rows, step_rows)
+        for ref, lanes in ((in_hbm, pl.ds(0, wide_in)), (out_hbm, pl.ds(wide_in, wide_out))):
+            pltpu.make_async_remote_copy(
+                src_ref=ref.at[rows_, :], dst_ref=held.at[f, rows_, lanes], send_sem=sem, recv_sem=recv_sem.at[f, part],
+                device_id=peer, device_id_type=MESH,
+            ).start()
+
     def arrived(shard, part):
         move(shard, part, to_twin, send_sem).wait_recv()
 
-    def part_of(q):
-        return (q % 2) * 2 + (q // 2) * (1 - 2 * side_y) + side_y
-
-    pl.semaphore_wait(barrier, 7)
-    loads[0].wait()
-    loads[1].wait()
-
+    pl.semaphore_wait(barrier, 8)
     for q in range(PARTS):
 
         @pl.when(depth == 0)
         def _():
-            move(f, part_of(q), to_outer, edge_sem).start()
-
-        if q < 3:
-            send(f, part_of(q), to_east, to_west)
-        send(f, part_of(q), to_twin)
+            first_send(q, to_outer, edge_sem)
+
+        for peer in (to_east, to_west, to_far, to_twin):
+            first_send(q, peer, send_sem)
     tell(0)
+    for load in loads:
+        load.start()
 
     def near(h_, q):
-        part = part_of(q)
+        part = q
         first, second = name(west, h_, c), name(east, h_, c)
-        arrived(first, part)
-        if q == 0:
-            send(first, part, to_east)
-        if q == 1:
-            send(first, part, to_pair)
-        send(first, part, to_twin)
-        arrived(second, part)
-        if q == 1:
-            send(second, part, to_west, to_pair)
-        send(second, part, to_twin)
+        for shard in (first, second):
+            arrived(shard, part)
+            send(shard, part, to_twin)
 
     def remote(h_, q):
-        shard, part = name(far, h_, c), part_of(q)
+        shard, part = name(far, h_, c), q
         arrived(shard, part)
-        if q < 2:
-            send(shard, part, to_pair)
         send(shard, part, to_twin)
 
     across = name(x, 1 - h, c)
 
     for t in range(2 * PARTS):
-        if t < 3:
+        if t < 4:
             near(h, t)
         q = t - 2 * depth
 
         @pl.when(jnp.logical_and(q >= 0, q < PARTS))
         def _():
-            part = part_of(q)
+            part = q
             arrived(across, part)
 
             @pl.when(depth < 2)
             def _():
                 move(across, part, to_inner, inner_sem).start()
 
-            @pl.when(q < 3)
-            def _():
-                send(across, part, to_east, to_west)
-
-            send(across, part, to_twin)
-
-        if t == 3:
-            hear_and_tell(0)
-        if t == 5:
-            hear_and_tell(1)
+            send(across, part, to_east, to_west, to_far, to_twin)
+
+        if t < ROUNDS - 1:
+            hear_and_tell(t)
 
     def use(shard):
         a = hidden[:, pl.ds(pl.multiple_of(shard * wide_in, 128), wide_in)]
@@ -234,37 +222,36 @@
     nt = (((1,), (1,)), ((), ()))
     acc_in[...] = jnp.zeros_like(acc_in)
     acc_out[...] = jnp.zeros_like(acc_out)
-    remote(h, 0)
-    remote(h, 1)
-    hear_and_tell(2)
-    near(1 - h, 0)
-    near(h, 3)
-    hear_and_tell(3)
-    near(1 - h, 1)
-    remote(h, 2)
-    remote(h, 3)
-    near(1 - h, 2)
-    hear_and_tell(4)
-    remote(1 - h, 0)
-    remote(1 - h, 1)
+    for load in loads[4:]:
+        load.wait()
     prepare_tables(
         piece_ref[...].astype(jnp.float32), target_ref[...].astype(jnp.float32), slot_ref[...].astype(jnp.float32),
         select, label_part, turn, spread_label,
     )
-    loads[2].wait()
-    loads[3].wait()
+    for load in loads[:4]:
+        load.wait()
+    remote(h, 0)
+    remote(h, 1)
+    remote(h, 2)
+    remote(h, 3)
+    near(1 - h, 0)
+    near(1 - h, 1)
+    near(1 - h, 2)
+    near(1 - h, 3)
     for x_ in (x, west, east, far):
         use(name(x_, h, c))
-    hear_and_tell(5)
-    near(1 - h, 3)
+    for x_ in (x, west, east, far):
+        take(name(x_, h, 1 - c))
+    for x_ in (x, west, east):
+        use(name(x_, 1 - h, c))
+    remote(1 - h, 0)
+    remote(1 - h, 1)
     remote(1 - h, 2)
     remote(1 - h, 3)
-    for x_ in (x, west, east, far):
-        take(name(x_, h, 1 - c))
-    for x_ in (x, west, east, far):
-        use(name(x_, 1 - h, c))
-    for x_ in (x, west, east, far):
+    for x_ in (x, west, east):
         take(name(x_, 1 - h, 1 - c))
+    use(name(far, 1 - h, c))
+    take(name(far, 1 - h, 1 - c))
     hear(6)
 
     def drain(ref, count, sem):
@@ -287,9 +274,7 @@
 
     keep(packed.at[SHIFT], owned_rows.at[SHIFT], 0)
 
-    @pl.loop(1, EACH)
-    def _(j):
-        k = (SHIFT + j) % EACH
+    for k in sorted(range(EACH), key=lambda k: -abs(k - SHIFT))[:-1]:
         post(packed.at[k], owned_rows.at[k], ((d + k + ND - SHIFT) % ND, f), 0)
 
     drain(owned_rows, EACH, swap_recv.at[0])
@@ -344,18 +329,20 @@
     def term(o):
         return terms.at[o // 2, o % 2]
 
-    @pl.when(at_home)
-    def _():
-        keep(term(d), gathered.at[mine], 2)
-
-    @pl.when(jnp.logical_not(at_home))
-    def _():
-        post(term(d), gathered.at[mine], (d, column), 2)
-
-    @pl.loop(1, ND)
+    start = d + jnp.where(at_home, ND // 2, 0)
+
+    @pl.loop(0, ND)
     def _(j):
-        o = (d + j) % ND
-        post(term(o), gathered.at[mine], (o, column), 2)
+        o = (start + j) % ND
+        here_too = jnp.logical_and(at_home, o == d)
+
+        @pl.when(here_too)
+        def _():
+            keep(term(o), gathered.at[mine], 2)
+
+        @pl.when(jnp.logical_not(here_too))
+        def _():
+            post(term(o), gathered.at[mine], (o, column), 2)
 
     drain(gathered, ND, swap_recv.at[2])
     total = jnp.sum(gathered[...].astype(jnp.float32), axis=0)
@@ -394,9 +381,12 @@
     total = pl.pallas_call(
         gram_kernel,
         out_shape=jax.ShapeDtypeStruct((GR // ND, 4096 // GROUP), f32),
-        in_specs=[anywhere] * 4 + [vmem] * 3,
+        in_specs=[anywhere] * 7,
         out_specs=vmem,
         scratch_shapes=[
+            pltpu.VMEM(piece_of.shape, jnp.int32),
+            pltpu.VMEM(owner_dp.shape, jnp.int32),
+            pltpu.VMEM(owner_slot.shape, jnp.int32),
             pltpu.VMEM(hidden_in.shape, bf16),
             pltpu.VMEM(out_grads.shape, bf16),
             pltpu.VMEM((GROUP, width, wide), bf16),
@@ -413,7 +403,7 @@
             pltpu.VMEM((2 * GROUP, 2 * OWN, 128), bf16),
             pltpu.VMEM((GR // 8, 2, 8, 128), bf16),
             pltpu.VMEM((ND, 8, 128), bf16),
-            pltpu.SemaphoreType.DMA((4,)),
+            pltpu.SemaphoreType.DMA((7,)),
             pltpu.SemaphoreType.DMA((GROUP, PARTS)),
             pltpu.SemaphoreType.DMA,
             pltpu.SemaphoreType.DMA,

time: 64.9 us -> 63.9 us (0.985)
  Pallas kernels: 63.4 us -> 62.4 us
    pallas_call x1, Pallas kernels: 63.4 us -> 62.4 us  [on_device(): pl.pallas_call(gram_kernel, out_shape=jax.ShapeDtypeStruct((GR // ND, 409...]
where the time goes in v5:
time: 63.9 us; the launch traced here: 63.7 us
  Pallas kernels  62.4 us (98%)
  other arithmetic  1.28 us (2%)
    pallas_call x1, Pallas kernels, on_device(): pl.pallas_call(gram_kernel, out_shape=jax.ShapeDtypeStruct((GR // ND, 409...  62.4 us

profile of v5, /device:TPU:1, one launch (start us, length us, event | category | flops | bytes accessed | tf_op | source)
XLA Modules:
  0.0 63.7 jit_solution(3003250873365803136)
XLA Ops:
  0.0 62.4 %gram.1 = f32[4,256]{1,0:T(4,128)} custom-call(bf16[128,14336]{1,0:T(8,128)(2,1)} %hidden_hbm.1, bf16[128,4096]{1,0:T(8,128)(2,1)} %grads_hbm.1, bf16[64,896]{1,0:T(8,128)(2,1)} %bitcast.2, bf16[64,256]{1,0:T(8,128)(2,1)} %bitcast.3, s32[1,128]{1,0:T(1,128)} %piece_hbm.1, s32[1,48]{1,0:T(1,128)} %target_hbm.1, s32[1,48]{1,0:T(1,128)} %slot_hbm.1), custom_call_target="tpu_custom_call" | custom-call | tf_op jit(solution)/shard_map/gram/pallas_call | solution.py:381
  62.5 1.3 %broadcast_multiply_fusion = f32[4,256]{1,0:T(4,128)} fusion(f32[4,256]{1,0:T(4,128)} %gram.1), kind=kLoop, calls=%fused_computation | loop fusion | flops 1024 | bytes 8192 | tf_op jit(solution)/shard_map/mul | solution.py:418

commit v6 on v5

--- a/solution.py
+++ b/solution.py
@@ -78,7 +78,7 @@
 def gram_kernel(
     hidden_hbm, grads_hbm, in_hbm, out_hbm, piece_hbm, target_hbm, slot_hbm, result_ref,
     piece_ref, target_ref, slot_ref, hidden, grads, held, acc_in, acc_out, select, label_part, turn, spread_label, low, packed, owned_rows,
-    feature, mixed, terms, gathered, load_sem, recv_sem, send_sem, edge_sem, inner_sem, swap_send, swap_recv, round_sem,
+    feature, mixed, terms, gathered, load_sem, recv_sem, send_sem, edge_sem, inner_sem, swap_send, swap_recv, round_sem, left_recv,
 ):
     d, f = lax.axis_index("dp"), lax.axis_index("fsdp")
     p, y = d // NY, d % NY
@@ -299,11 +299,22 @@
     here = name(x, (y + p) % 2, c)
     keep(feature.at[here], mixed.at[2 * here], 1)
     keep(feature.at[0], mixed.at[2 * here + 1], 1)
+    post(feature.at[0], mixed.at[2 * here + 1], to_twin, 1)
+    same_core = range(GROUP - 2, 0, -2)
+    for other in same_core:
+        back = (NX - other // 4) % NX * 2 + (other // 2) % 2
+        pltpu.make_async_remote_copy(
+            src_ref=feature.at[0], dst_ref=mixed.at[2 * here + 1], send_sem=swap_send.at[1], recv_sem=left_recv.at[back],
+            device_id=member(other)[0], device_id_type=MESH,
+        ).start()
     for other in range(GROUP - 1, 0, -1):
         peer, columns = member(other)
         post(feature.at[columns], mixed.at[2 * here], peer, 1)
-        post(feature.at[0], mixed.at[2 * here + 1], peer, 1)
-    drain(mixed, 2 * GROUP, swap_recv.at[1])
+    for other in sorted(same_core, key=lambda o: (o // 4) % 2 + 2 * (o // 8 % 2) * (1 - (o // 4) % 2) + (o // 2) % 2):
+        block = mixed.at[2 * member(other)[1] + 1]
+        pltpu.make_async_copy(block, block, left_recv.at[other // 2]).wait()
+        post(block, block, to_twin, 1)
+    drain(mixed, 2 * GROUP - 7, swap_recv.at[1])
 
     both = mixed[...].astype(jnp.float32).reshape(GROUP, 2, 2, OWN, 128)
     tn = (((0,), (0,)), ((), ()))
@@ -411,6 +422,7 @@
             pltpu.SemaphoreType.DMA((3,)),
             pltpu.SemaphoreType.DMA((3,)),
             pltpu.SemaphoreType.REGULAR((ROUNDS,)),
+            pltpu.SemaphoreType.DMA((GROUP // 2,)),
         ],
         compiler_params=pltpu.CompilerParams(collective_id=0, has_side_effects=True),
         name="gram",

time: 63.9 us -> 63.7 us (level)
  no operation moved by 1% of the time
where the time goes in v6:
time: 63.7 us; the launch traced here: 63.5 us
  Pallas kernels  62.3 us (98%)
  other arithmetic  1.28 us (2%)
    pallas_call x1, Pallas kernels, on_device(): pl.pallas_call(gram_kernel, out_shape=jax.ShapeDtypeStruct((GR // ND, 409...  62.3 us
    mul x1, other arithmetic, on_device(): return total * (1.0 / math.sqrt(OWN * ND * GROUP))  1.28 us

profile of v6, /device:TPU:1, one launch (start us, length us, event | category | flops | bytes accessed | tf_op | source)
XLA Modules:
  0.0 63.5 jit_solution(6797388877473756730)
XLA Ops:
  0.0 62.3 %gram.1 = f32[4,256]{1,0:T(4,128)} custom-call(bf16[128,14336]{1,0:T(8,128)(2,1)} %hidden_hbm.1, bf16[128,4096]{1,0:T(8,128)(2,1)} %grads_hbm.1, bf16[64,896]{1,0:T(8,128)(2,1)} %bitcast.2, bf16[64,256]{1,0:T(8,128)(2,1)} %bitcast.3, s32[1,128]{1,0:T(1,128)} %piece_hbm.1, s32[1,48]{1,0:T(1,128)} %target_hbm.1, s32[1,48]{1,0:T(1,128)} %slot_hbm.1), custom_call_target="tpu_custom_call" | custom-call | tf_op jit(solution)/shard_map/gram/pallas_call | solution.py:392
  62.3 1.3 %broadcast_multiply_fusion = f32[4,256]{1,0:T(4,128)} fusion(f32[4,256]{1,0:T(4,128)} %gram.1), kind=kLoop, calls=%fused_computation | loop fusion | flops 1024 | bytes 8192 | tf_op jit(solution)/shard_map/mul | solution.py:430
